TPU v7x, 256 devices: a whole 4x4x8 slice. The times are simulated.
256 devices in a mesh: dp: 16 (over x_hi, y, core), hid: 16 (over x_lo, z).
Axes of the slice: x: 4 (x_hi: 2, x_lo: 2; x = x_hi * 2 + x_lo), y: 4, z: 8, core: 2. Of those that a mesh axis runs over, the one named last changes fastest.
Arguments:
- tokens: bfloat16 [2048, 4096], P('dp', 'hid'), may hold values from -6 to 6
- expert_ids: int32 [2048, 2], P('dp'), may hold values from 0 to 7, all different within a row; in each aligned block of 128 rows (0 to 127, 128 to 255, ...) at most 48 rows name the same one
- gate_levels: int32 [2048, 2], P('dp'), may hold values from 1 to 255
- w_gate: bfloat16 [4096, 114688], P(None, ('dp', 'hid')), may hold values from -0.09375 to 0.09375
- w_up: bfloat16 [4096, 114688], P(None, ('dp', 'hid')), may hold values from -0.09375 to 0.09375
- w_down: bfloat16 [114688, 4096], P(('dp', 'hid')), may hold values from -0.046875 to 0.046875
Outputs:
- mixed: bfloat16 [2048, 4096], P('dp', 'hid')
Inputs may be any that keep to these rules, and one draw needn't show every extreme that they name: `expert_ids`: each row names two different experts. Among the 128 rows of one index of dp no expert is named by more than 48 rows, and in some such block one expert is named by exactly 48 rows.
All inputs are finite; a program needn't handle non-finite values.
Results may differ from a plain program's by a relative error of at most 0.019.
Values may be sent and summed in bfloat16 or wider, within the bound.
A program may use at most 64 MiB of HBM per device.

v0:
```python
import jax
import jax.numpy as jnp
from jax import lax
from jax.sharding import PartitionSpec as P

EXPERTS = 8


def local(tokens, expert_ids, gate_levels, w_gate, w_up, w_down):
    devices_dp = lax.axis_size("dp")
    halves_each = devices_dp // EXPERTS
    tok_rows = expert_ids.shape[0]
    capacity = 3 * tok_rows // 8
    flat_ids = expert_ids.reshape(-1)
    total = flat_ids.shape[0]
    one_hot = (flat_ids[:, None] == jnp.arange(EXPERTS, dtype=jnp.int32)[None, :]).astype(jnp.int32)
    earlier = jnp.cumsum(one_hot, axis=0) - one_hot
    slot_of = jnp.sum(earlier * one_hot, axis=1)
    dest_row = flat_ids * capacity + slot_of
    src_token = (
        jnp.full((EXPERTS * capacity,), -1, jnp.int32)
        .at[dest_row]
        .set(jnp.arange(total, dtype=jnp.int32) // 2)
    )
    filled = src_token >= 0
    src_index = jnp.maximum(src_token, 0)
    levels = gate_levels.astype(jnp.float32)
    gate_frac = levels / jnp.sum(levels, axis=1, keepdims=True)
    full_rows = lax.all_gather(tokens, "hid", axis=1, tiled=True)
    width = full_rows.shape[1]
    picked = jnp.where(filled[:, None], full_rows[src_index], jnp.zeros((), full_rows.dtype))
    picked = picked.reshape(EXPERTS, 1, capacity, width)
    spread = jnp.broadcast_to(picked, (EXPERTS, halves_each, capacity, width))
    received = lax.all_to_all(
        spread.reshape(devices_dp, capacity, width), "dp", split_axis=0, concat_axis=0, tiled=True
    )
    received = received.reshape(devices_dp * capacity, full_rows.shape[1])
    gate = jnp.dot(received, w_gate, preferred_element_type=jnp.float32)
    up = jnp.dot(received, w_up, preferred_element_type=jnp.float32)
    hidden = (jax.nn.silu(gate) * up).astype(jnp.bfloat16)
    partial_out = jnp.dot(hidden, w_down, preferred_element_type=jnp.float32)
    summed = lax.psum_scatter(
        partial_out.astype(jnp.bfloat16), "hid", scatter_dimension=1, tiled=True
    )
    returned = lax.all_to_all(
        summed.reshape(devices_dp, capacity, summed.shape[1]),
        "dp",
        split_axis=0,
        concat_axis=0,
        tiled=True,
    )
    halves_sum = (
        returned.reshape(EXPERTS, halves_each, capacity, summed.shape[1])
        .astype(jnp.float32)
        .sum(axis=1)
    )
    halves_sum = halves_sum.reshape(EXPERTS * capacity, summed.shape[1])
    chosen = halves_sum[dest_row] * gate_frac.reshape(-1)[:, None]
    return chosen.reshape(tok_rows, 2, summed.shape[1]).sum(axis=1).astype(jnp.bfloat16)


def solution(mesh):
    placed = (
        P("dp", "hid"),
        P("dp", None),
        P("dp", None),
        P(None, ("dp", "hid")),
        P(None, ("dp", "hid")),
        P(("dp", "hid"), None),
    )
    return jax.shard_map(
        local, mesh=mesh, in_specs=placed, out_specs=P("dp", "hid"), check_vma=False
    )
```

profile of v0, /device:TPU:1, one launch (start us, length us, event | category | flops | bytes accessed | tf_op | source)
XLA Modules:
  0.0 299.5 jit_solution(11578916369394543417)
XLA Ops:
  6.5 0.0 all-gather.2.cloned.1.call-start
  6.5 0.7 all-gather.2.cloned.1.call-update
  7.3 0.0 reduce-scatter.2.cloned.1.call-start
  7.3 0.8 copy.9
  8.1 0.1 eq.29
  8.2 0.1 eq.25
  8.4 0.6 reduce-window.6
  9.0 0.2 slice_reduce_fusion
  9.2 0.7 broadcast_multiply_fusion
  9.9 0.1 copy.8
  10.0 0.1 mul.37
  10.2 0.1 fusion.2
  10.3 1.4 scatter_custom_fusion
  11.7 0.1 broadcast_in_dim.31
  11.8 54.8 %all-gather.2.cloned.1.call-done = bf16[128,4096]{1,0:T(8,128)(2,1)} async-done(((bf16[128,256]{1,0:T(8,128)(2,1)}), bf16[128,4096]{1,0:T(8,128)(2,1)}) %all-gather.2.cloned.1.call-update) | async-done | bytes 1048592 | tf_op jit(solution)/shard_map/all_gather | solution.py:29
  66.6 8.9 %gather_fusion = bf16[384,4096]{1,0:T(8,128)(2,1)S(1)} fusion(bf16[128,4096]{1,0:T(8,128)(2,1)} %all-gather.2.cloned.1.call-done, s32[1024]{0:T(1024)S(1)} %pad_clamp_fusion.1), kind=kCustom, calls=%fused_computation | custom fusion | bytes 6292992 | tf_op jit(solution)/shard_map/gather | solution.py:31
  75.5 0.3 broadcast_select_fusion
  75.8 0.8 broadcast_in_dim.35
  76.6 0.0 copy-start.2
  76.6 91.2 %all_to_all.10 = bf16[16,48,4096]{2,1,0:T(8,128)(2,1)S(1)} all-to-all(bf16[16,48,4096]{2,1,0:T(8,128)(2,1)S(1)} %bitcast.23), channel_id=1, replica_groups=mesh['dp'=16,'hid'=16] {'dp'}, dimensions={0} | all-to-all | bytes 12582912 | tf_op jit(solution)/shard_map/all_to_all | solution.py:34
  167.8 0.0 copy-start
  167.8 2.7 copy-done
  170.4 0.0 copy-done.2
  170.4 3.1 %fusion.7 = f32[768,448]{0,1:T(8,128)S(1)} fusion(bf16[768,4096]{1,0:T(8,128)(2,1)S(1)} %bitcast.26, bf16[4096,448]{0,1:T(8,128)(2,1)S(1)} %copy-done.2), kind=kOutput, calls=%fused_computation.31 | convolution fusion | flops 2818572288 | bytes 11337728 | tf_op jit(solution)/shard_map/dot_general | solution.py:38
  173.5 15.9 %convolution_convert_fusion = bf16[768,4096]{1,0:T(8,128)(2,1)} fusion(bf16[448,4096]{1,0:T(8,128)(2,1)} %param.11, bf16[768,4096]{1,0:T(8,128)(2,1)} %bitcast.27, bf16[4096,448]{0,1:T(8,128)(2,1)} %param.10, f32[768,448]{0,1:T(8,128)S(1)} %fusion.7), kind=kOutput, calls=%fused_computation.3 | convolution fusion | flops 5642354688 | bytes 21299200 | tf_op jit(solution)/shard_map/dot_general | solution.py:41
  189.5 0.0 copy-start.1
  189.5 0.0 reduce-scatter.2.cloned.1.call-update
  189.5 75.5 %reduce-scatter.2.cloned.1.call-done = bf16[768,256]{1,0:T(8,128)(2,1)} async-done(((bf16[768,4096]{1,0:T(8,128)(2,1)}), bf16[768,256]{1,0:T(8,128)(2,1)}) %reduce-scatter.2.cloned.1.call-update) | async-done | bytes 393232 | tf_op jit(solution)/shard_map/reduce_scatter | solution.py:42
  264.9 15.7 %all-to-all-start.1 = ((bf16[16,48,256]{2,1,0:T(8,128)(2,1)}), bf16[16,48,256]{2,1,0:T(8,128)(2,1)S(1)}, u32[]{:S(2)}, u32[]{:S(2)}) async-start(bf16[16,48,256]{2,1,0:T(8,128)(2,1)} %bitcast.28), calls=%async_computation.2 | async-start | bytes 786432 | tf_op jit(solution)/shard_map/all_to_all | solution.py:45
  280.7 0.0 copy-done.1
  280.7 0.1 copy.11
  280.8 9.6 %all-to-all-done.1 = bf16[16,48,256]{2,1,0:T(8,128)(2,1)S(1)} async-done(((bf16[16,48,256]{2,1,0:T(8,128)(2,1)}), bf16[16,48,256]{2,1,0:T(8,128)(2,1)S(1)}, u32[]{:S(2)}, u32[]{:S(2)}) %all-to-all-start.1) | async-done | bytes 393248 | tf_op jit(solution)/shard_map/all_to_all | solution.py:45
  290.4 0.1 convert_reduce_fusion
  290.5 1.0 gather_fusion.1
  291.5 0.1 gather.13
  291.6 1.0 multiply_reduce_fusion
  (11 shorter events, 0.1 us)
Async XLA Ops:
  6.5 60.1 %all-gather.2.cloned.1.call-start = ((), (), s32[]{:S(2)}) async-start(), calls=%async_computation.3 | async-start | bytes 1114112 | tf_op jit(solution)/shard_map/all_gather | solution.py:29
  7.3 257.7 %reduce-scatter.2.cloned.1.call-start = ((), (), s32[]{:S(2)}) async-start(), calls=%async_computation.4 | async-start | bytes 6684672 | tf_op jit(solution)/shard_map/reduce_scatter | solution.py:42
  76.6 93.9 %copy-start.2 = (bf16[4096,448]{0,1:T(8,128)(2,1)S(1)}, bf16[4096,448]{0,1:T(8,128)(2,1)}, u32[]{:S(2)}) copy-start(bf16[4096,448]{0,1:T(8,128)(2,1)} %param.9) | copy-start | bytes 11010052
  167.8 2.7 copy-start
  189.5 91.2 %copy-start.1 = (s32[128,2]{0,1:T(2,128)S(1)}, s32[128,2]{0,1:T(2,128)}, u32[]{:S(2)}) copy-start(s32[128,2]{0,1:T(2,128)} %param.8) | copy-start | bytes 3076
  264.9 25.5 %all-to-all-start.1 = ((bf16[16,48,256]{2,1,0:T(8,128)(2,1)}), bf16[16,48,256]{2,1,0:T(8,128)(2,1)S(1)}, u32[]{:S(2)}, u32[]{:S(2)}) async-start(bf16[16,48,256]{2,1,0:T(8,128)(2,1)} %bitcast.28), calls=%async_computation.2 | async-start | bytes 786432 | tf_op jit(solution)/shard_map/all_to_all | solution.py:45
Sparse Core Ops, SparseCore 0:
  9.0 57.5 all-gather.1
  189.6 75.2 reduce-scatter.1
where the time goes:
time: 300 us; the launch traced here: 299 us
  waiting for transfers between devices  141 us (47%)
  blocking collectives  91.2 us (30%)
  matrix products  19 us (6%)
  local copies, waits for them, and re-layouts  16.6 us (6%)
  starting transfers between devices  15.8 us (5%)
  between operations  13.5 us (4%)
    all_to_all x1, blocking collectives, local(): lax.all_to_all(spread.reshape(devices_dp, capacity, width), 'dp', split_a...  91.2 us
    reduce_scatter x1, waiting for transfers between devices, local(): lax.psum_scatter(partial_out.astype(jnp.bfloat16), 'hid', scatter_dimensi...  75.5 us
    all_gather x1, waiting for transfers between devices, local(): full_rows = lax.all_gather(tokens, 'hid', axis=1, tiled=True)  54.8 us
    dot_general x1, matrix products, local(): partial_out = jnp.dot(hidden, w_down, preferred_element_type=jnp.float32)  15.9 us
    all_to_all x1, starting transfers between devices, local(): lax.all_to_all(summed.reshape(devices_dp, capacity, summed.shape[1]), 'dp...  15.7 us
    all_to_all x1, waiting for transfers between devices, local(): lax.all_to_all(summed.reshape(devices_dp, capacity, summed.shape[1]), 'dp...  9.6 us
    gather x1, local copies, waits for them, and re-layouts, local(): full_rows[src_index]  8.87 us
  transfers between devices with their start and end apart: 3, of which 3 were waited for; matrix products, arithmetic and copies ran while one was open for 2% of the time, Pallas kernels for 0%

commit v1 on v0

--- a/solution.py
+++ b/solution.py
@@ -26,7 +26,9 @@
     src_index = jnp.maximum(src_token, 0)
     levels = gate_levels.astype(jnp.float32)
     gate_frac = levels / jnp.sum(levels, axis=1, keepdims=True)
-    full_rows = lax.all_gather(tokens, "hid", axis=1, tiled=True)
+    full_rows = jnp.concatenate(
+        lax.all_to_all(jnp.stack([tokens] * lax.axis_size("hid")), "hid", 0, 0), axis=1
+    )
     width = full_rows.shape[1]
     picked = jnp.where(filled[:, None], full_rows[src_index], jnp.zeros((), full_rows.dtype))
     picked = picked.reshape(EXPERTS, 1, capacity, width)

time: 300 us -> 264 us (0.88)
  waiting for transfers between devices: 141 us -> 104 us
  starting transfers between devices: 15.8 us -> 25.9 us
  blocking collectives: 91.2 us -> 82.2 us
    all_gather x1 -> x0, waiting for transfers between devices: 54.8 us -> none  [local(): full_rows = lax.all_gather(tokens, 'hid', axis=1, tiled=True)]
    all_to_all x0 -> x1, waiting for transfers between devices: none -> 21 us  [local(): lax.all_to_all(jnp.stack([tokens] * lax.axis_size('hid')), 'hid', 0, 0)]
    all_to_all x0 -> x1, starting transfers between devices: none -> 10 us  [local(): lax.all_to_all(jnp.stack([tokens] * lax.axis_size('hid')), 'hid', 0, 0)]
    all_to_all x1, blocking collectives: 91.2 us -> 82.2 us  [local(): lax.all_to_all(spread.reshape(devices_dp, capacity, width), 'dp', split_a...]
    gather x1, local copies, waits for them, and re-layouts: 8.87 us -> 4.04 us  [local(): full_rows[src_index]]
where the time goes in v1:
time: 264 us; the launch traced here: 263 us
  waiting for transfers between devices  104 us (39%)
  blocking collectives  82.2 us (31%)
  starting transfers between devices  25.9 us (10%)
  matrix products  19 us (7%)
  local copies, waits for them, and re-layouts  13.8 us (5%)
  between operations  13.5 us (5%)
  other arithmetic  4.72 us (2%)
    all_to_all x1, blocking collectives, local(): lax.all_to_all(spread.reshape(devices_dp, capacity, width), 'dp', split_a...  82.2 us
    reduce_scatter x1, waiting for transfers between devices, local(): lax.psum_scatter(partial_out.astype(jnp.bfloat16), 'hid', scatter_dimensi...  73.4 us
    all_to_all x1, waiting for transfers between devices, local(): lax.all_to_all(jnp.stack([tokens] * lax.axis_size('hid')), 'hid', 0, 0)  21 us
    dot_general x1, matrix products, local(): partial_out = jnp.dot(hidden, w_down, preferred_element_type=jnp.float32)  15.9 us
    all_to_all x1, starting transfers between devices, local(): lax.all_to_all(summed.reshape(devices_dp, capacity, summed.shape[1]), 'dp...  15.8 us
    all_to_all x1, starting transfers between devices, local(): lax.all_to_all(jnp.stack([tokens] * lax.axis_size('hid')), 'hid', 0, 0)  10 us
    all_to_all x1, waiting for transfers between devices, local(): lax.all_to_all(summed.reshape(devices_dp, capacity, summed.shape[1]), 'dp...  9.6 us
  transfers between devices with their start and end apart: 3, of which 3 were waited for; matrix products, arithmetic and copies ran while one was open for 2% of the time, Pallas kernels for 0%

profile of v1, /device:TPU:1, one launch (start us, length us, event | category | flops | bytes accessed | tf_op | source)
XLA Modules:
  0.0 263.1 jit_solution(9672616327806192865)
XLA Ops:
  6.5 1.9 stack.2
  8.5 10.0 %all-to-all-start = ((bf16[16,128,256]{2,1,0:T(8,128)(2,1)}), bf16[16,128,256]{2,1,0:T(8,128)(2,1)S(1)}, u32[]{:S(2)}, u32[]{:S(2)}) async-start(bf16[16,128,256]{2,1,0:T(8,128)(2,1)} %stack.2), calls=%async_computation | async-start | bytes 2097152 | tf_op jit(solution)/shard_map/all_to_all | solution.py:30
  18.5 0.0 reduce-scatter.2.cloned.1.call-start
  18.6 0.8 copy.13
  19.3 0.1 eq.29
  19.5 0.1 eq.25
  19.6 0.6 reduce-window.6
  20.2 0.2 slice_reduce_fusion
  20.5 0.7 broadcast_multiply_fusion
  21.2 0.1 copy.12
  21.3 0.1 mul.37
  21.4 0.1 fusion.2
  21.5 1.4 scatter_custom_fusion
  23.0 0.1 broadcast_in_dim.31
  23.1 21.0 %all-to-all-done = bf16[16,128,256]{2,1,0:T(8,128)(2,1)S(1)} async-done(((bf16[16,128,256]{2,1,0:T(8,128)(2,1)}), bf16[16,128,256]{2,1,0:T(8,128)(2,1)S(1)}, u32[]{:S(2)}, u32[]{:S(2)}) %all-to-all-start) | async-done | bytes 1048608 | tf_op jit(solution)/shard_map/all_to_all | solution.py:30
  44.1 0.1 copy.17
  44.2 4.0 %gather_fusion = bf16[384,4096]{1,0:T(8,128)(2,1)} fusion(bf16[128,4096]{1,0:T(8,128)(2,1)S(1)} %bitcast.26, s32[1024]{0:T(1024)S(1)} %pad_clamp_fusion.1), kind=kCustom, calls=%fused_computation | custom fusion | bytes 6292992 | tf_op jit(solution)/shard_map/gather | solution.py:33
  48.2 2.2 broadcast_select_fusion
  50.4 0.8 broadcast_in_dim.35
  51.2 0.0 copy-start.2
  51.2 82.2 %all_to_all.15 = bf16[16,48,4096]{2,1,0:T(8,128)(2,1)S(1)} all-to-all(bf16[16,48,4096]{2,1,0:T(8,128)(2,1)S(1)} %bitcast.27), channel_id=1, replica_groups=mesh['dp'=16,'hid'=16] {'dp'}, dimensions={0} | all-to-all | bytes 12582912 | tf_op jit(solution)/shard_map/all_to_all | solution.py:36
  133.4 0.0 copy-start
  133.4 2.7 %copy-done = bf16[16,48,4096]{2,1,0:T(8,128)(2,1)} copy-done((bf16[16,48,4096]{2,1,0:T(8,128)(2,1)}, bf16[16,48,4096]{2,1,0:T(8,128)(2,1)S(1)}, u32[]{:S(2)}) %copy-start) | copy-done | bytes 6291480
  136.0 0.0 copy-done.2
  136.0 3.1 %fusion.7 = f32[768,448]{0,1:T(8,128)S(1)} fusion(bf16[768,4096]{1,0:T(8,128)(2,1)S(1)} %bitcast.30, bf16[4096,448]{0,1:T(8,128)(2,1)S(1)} %copy-done.2), kind=kOutput, calls=%fused_computation.31 | convolution fusion | flops 2818572288 | bytes 11337728 | tf_op jit(solution)/shard_map/dot_general | solution.py:40
  139.1 15.9 %convolution_convert_fusion = bf16[768,4096]{1,0:T(8,128)(2,1)} fusion(bf16[448,4096]{1,0:T(8,128)(2,1)} %param.11, bf16[768,4096]{1,0:T(8,128)(2,1)} %bitcast.31, bf16[4096,448]{0,1:T(8,128)(2,1)} %param.10, f32[768,448]{0,1:T(8,128)S(1)} %fusion.7), kind=kOutput, calls=%fused_computation.3 | convolution fusion | flops 5642354688 | bytes 21299200 | tf_op jit(solution)/shard_map/dot_general | solution.py:43
  155.1 0.0 copy-start.1
  155.1 0.0 reduce-scatter.2.cloned.1.call-update
  155.1 73.4 %reduce-scatter.2.cloned.1.call-done = bf16[768,256]{1,0:T(8,128)(2,1)} async-done(((bf16[768,4096]{1,0:T(8,128)(2,1)}), bf16[768,256]{1,0:T(8,128)(2,1)}) %reduce-scatter.2.cloned.1.call-update) | async-done | bytes 393232 | tf_op jit(solution)/shard_map/reduce_scatter | solution.py:44
  228.5 15.8 %all-to-all-start.2 = ((bf16[16,48,256]{2,1,0:T(8,128)(2,1)}), bf16[16,48,256]{2,1,0:T(8,128)(2,1)S(1)}, u32[]{:S(2)}, u32[]{:S(2)}) async-start(bf16[16,48,256]{2,1,0:T(8,128)(2,1)} %bitcast.33), calls=%async_computation.3 | async-start | bytes 786432 | tf_op jit(solution)/shard_map/all_to_all | solution.py:47
  244.3 0.0 copy-done.1
  244.3 0.1 copy.16
  244.5 9.6 %all-to-all-done.2 = bf16[16,48,256]{2,1,0:T(8,128)(2,1)S(1)} async-done(((bf16[16,48,256]{2,1,0:T(8,128)(2,1)}), bf16[16,48,256]{2,1,0:T(8,128)(2,1)S(1)}, u32[]{:S(2)}, u32[]{:S(2)}) %all-to-all-start.2) | async-done | bytes 393248 | tf_op jit(solution)/shard_map/all_to_all | solution.py:47
  254.1 0.1 convert_reduce_fusion
  254.1 1.0 gather_fusion.1
  255.1 0.1 gather.13
  255.3 1.0 multiply_reduce_fusion
  (11 shorter events, 0.1 us)
Async XLA Ops:
  8.5 35.6 %all-to-all-start = ((bf16[16,128,256]{2,1,0:T(8,128)(2,1)}), bf16[16,128,256]{2,1,0:T(8,128)(2,1)S(1)}, u32[]{:S(2)}, u32[]{:S(2)}) async-start(bf16[16,128,256]{2,1,0:T(8,128)(2,1)} %stack.2), calls=%async_computation | async-start | bytes 2097152 | tf_op jit(solution)/shard_map/all_to_all | solution.py:30
  18.5 210.0 %reduce-scatter.2.cloned.1.call-start = ((), (), s32[]{:S(2)}) async-start(), calls=%async_computation.4 | async-start | bytes 6684672 | tf_op jit(solution)/shard_map/reduce_scatter | solution.py:44
  51.2 84.9 %copy-start.2 = (bf16[4096,448]{0,1:T(8,128)(2,1)S(1)}, bf16[4096,448]{0,1:T(8,128)(2,1)}, u32[]{:S(2)}) copy-start(bf16[4096,448]{0,1:T(8,128)(2,1)} %param.9) | copy-start | bytes 11010052
  133.4 2.7 %copy-start = (bf16[16,48,4096]{2,1,0:T(8,128)(2,1)}, bf16[16,48,4096]{2,1,0:T(8,128)(2,1)S(1)}, u32[]{:S(2)}) copy-start(bf16[16,48,4096]{2,1,0:T(8,128)(2,1)S(1)} %all_to_all.15) | copy-start | bytes 18874372
  155.1 89.2 %copy-start.1 = (s32[128,2]{0,1:T(2,128)S(1)}, s32[128,2]{0,1:T(2,128)}, u32[]{:S(2)}) copy-start(s32[128,2]{0,1:T(2,128)} %param.8) | copy-start | bytes 3076
  228.5 25.6 %all-to-all-start.2 = ((bf16[16,48,256]{2,1,0:T(8,128)(2,1)}), bf16[16,48,256]{2,1,0:T(8,128)(2,1)S(1)}, u32[]{:S(2)}, u32[]{:S(2)}) async-start(bf16[16,48,256]{2,1,0:T(8,128)(2,1)} %bitcast.33), calls=%async_computation.3 | async-start | bytes 786432 | tf_op jit(solution)/shard_map/all_to_all | solution.py:47
Sparse Core Ops, SparseCore 0:
  155.2 73.2 reduce-scatter.1
